TPU v7x, 32 devices: a whole 2x2x4 slice. The times are simulated.
32 devices in a mesh: ctx: 2 (over x), hs: 16 (over z, y, core).
Axes of the slice: x: 2, y: 2, z: 4, core: 2. Of those that a mesh axis runs over, the one named last changes fastest.
Arguments:
- key_rows: bfloat16 [16, 1024, 512], P('hs', 'ctx'), may hold values from -6 to 6
- value_rows: bfloat16 [16, 1024, 512], P('hs', 'ctx'), may hold values from -6 to 6
- query_rows: bfloat16 [16, 1024, 512], P('hs', 'ctx'), may hold values from -6 to 6
- step_rates: float32 [16, 1024], P('hs', 'ctx'), may hold values from 0.0003 to 0.003
- fast_gate: bfloat16 [16, 512, 512], P('hs', 'ctx'), may hold values from -0.25 to 0.25
- fast_up: bfloat16 [16, 512, 512], P('hs', 'ctx'), may hold values from -0.25 to 0.25
- fast_down: bfloat16 [16, 512, 512], P('hs', 'ctx'), may hold values from -0.25 to 0.25
- out_gain: float32 [2048], replicated, may hold values from 0.1 to 1.9
- gate_input: bfloat16 [1024, 4, 2048], P(('ctx', 'hs')), may hold values from -6 to 6
- out_weight: bfloat16 [2048, 1024], P('hs'), may hold values from -0.125 to 0.125
Outputs:
- layer_out: bfloat16 [1024, 4, 1024], P(('ctx', 'hs'))
All inputs are finite; a program needn't handle non-finite values.
Results may differ from a plain program's by a relative error of at most 0.01.
Values may be sent and summed in bfloat16 or wider, within the bound.
A program may use at most 64 MiB of HBM per device.

v0:
```python
import jax
import jax.numpy as jnp
from jax import lax
from jax.sharding import PartitionSpec as P

epsilon = 1e-06


def rescale_rows(weight, update):
    base = weight.astype(jnp.float32)
    moved = base + update
    factor = jnp.sqrt(jnp.mean(base * base, -1, keepdims=True) + epsilon) / jnp.sqrt(
        jnp.mean(moved * moved, -1, keepdims=True) + epsilon
    )
    return (moved * factor).astype(jnp.bfloat16)


def inner_rows(left, right):
    return lax.dot_general(
        left, right, (((0,), (0,)), ((), ())), preferred_element_type=jnp.float32
    )


def body(
    key_rows,
    value_rows,
    query_rows,
    step_rates,
    fast_gate,
    fast_up,
    fast_down,
    out_gain,
    gate_input,
    out_weight,
):
    key_row = key_rows[0]
    value_row = value_rows[0]
    query_row = query_rows[0]
    rate_row = step_rates[0]
    whole_gate, whole_up, whole_down = (
        lax.all_gather(fast_gate, "ctx", axis=1, tiled=True),
        lax.all_gather(fast_up, "ctx", axis=1, tiled=True),
        lax.all_gather(fast_down, "ctx", axis=1, tiled=True),
    )
    gate_fast = whole_gate[0]
    up_fast = whole_up[0]
    down_fast = whole_down[0]
    pre_gate = jnp.dot(key_row, gate_fast.T, preferred_element_type=jnp.float32)
    pre_up = jnp.dot(key_row, up_fast.T, preferred_element_type=jnp.float32)
    sig_gate = jax.nn.sigmoid(pre_gate)
    act_gate = pre_gate * sig_gate
    hidden = (act_gate * pre_up).astype(jnp.bfloat16)
    scaled = (rate_row[:, None] * value_row.astype(jnp.float32)).astype(jnp.bfloat16)
    grad_down = inner_rows(scaled, hidden)
    back_hidden = jnp.dot(scaled, down_fast, preferred_element_type=jnp.float32)
    back_gate = (back_hidden * pre_up * sig_gate * (1.0 + pre_gate * (1.0 - sig_gate))).astype(
        jnp.bfloat16
    )
    back_up = (back_hidden * act_gate).astype(jnp.bfloat16)
    grad_gate = inner_rows(back_gate, key_row)
    grad_up = inner_rows(back_up, key_row)
    grad_gate, grad_up, grad_down = (
        lax.psum_scatter(grad_gate, "ctx", scatter_dimension=0, tiled=True),
        lax.psum_scatter(grad_up, "ctx", scatter_dimension=0, tiled=True),
        lax.psum_scatter(grad_down, "ctx", scatter_dimension=0, tiled=True),
    )
    part_gate = rescale_rows(fast_gate[0], grad_gate)
    part_up = rescale_rows(fast_up[0], grad_up)
    part_down = rescale_rows(fast_down[0], grad_down)
    new_gate, new_up, new_down = (
        lax.all_gather(part_gate, "ctx", axis=0, tiled=True),
        lax.all_gather(part_up, "ctx", axis=0, tiled=True),
        lax.all_gather(part_down, "ctx", axis=0, tiled=True),
    )
    query_gate = jnp.dot(query_row, new_gate.T, preferred_element_type=jnp.float32)
    query_up = jnp.dot(query_row, new_up.T, preferred_element_type=jnp.float32)
    query_hidden = (jax.nn.silu(query_gate) * query_up).astype(jnp.bfloat16)
    head_out = jnp.dot(query_hidden, new_down.T, preferred_element_type=jnp.float32).astype(
        jnp.bfloat16
    )
    width_hs = lax.axis_size("hs")
    head_size = head_out.shape[1]
    token_count = head_out.shape[0] // width_hs
    blocks = head_out.reshape(width_hs, token_count, head_size)
    moved = lax.all_to_all(blocks, "hs", split_axis=0, concat_axis=2, tiled=True)
    seq_count = gate_input.shape[1]
    model_width = gate_input.shape[2]
    head_count = model_width // head_size
    mixed = moved.reshape(token_count, seq_count, head_count, head_size).astype(jnp.float32)
    square = jnp.mean(mixed * mixed, -1, keepdims=True)
    scaled_heads = mixed * lax.rsqrt(square + epsilon) * out_gain.reshape(head_count, head_size)
    normed = (
        scaled_heads.reshape(token_count, seq_count, model_width)
        * jax.nn.silu(gate_input.astype(jnp.float32))
    ).astype(jnp.bfloat16)
    flat_rows = normed.reshape(token_count * seq_count, model_width)
    out_cols = out_weight.shape[1]
    full_weight = lax.all_gather(out_weight, "hs", axis=0, tiled=True)
    result = jnp.dot(flat_rows, full_weight, preferred_element_type=jnp.float32)
    return result.astype(jnp.bfloat16).reshape(token_count, seq_count, out_cols)


def solution(mesh):
    return jax.shard_map(
        body,
        mesh=mesh,
        in_specs=(
            P("hs", "ctx", None),
            P("hs", "ctx", None),
            P("hs", "ctx", None),
            P("hs", "ctx"),
            P("hs", "ctx", None),
            P("hs", "ctx", None),
            P("hs", "ctx", None),
            P(),
            P(("ctx", "hs"), None, None),
            P("hs", None),
        ),
        out_specs=P(("ctx", "hs"), None, None),
        check_vma=False,
    )
```

profile of v0, /device:TPU:13, one launch (start us, length us, event | category | flops | bytes accessed | tf_op | source)
XLA Modules:
  0.0 156.4 jit_solution(564496590569999694)
XLA Ops:
  7.4 8.2 %all_gather.21 = bf16[1,512,512]{2,1,0:T(8,128)(2,1)S(1)} all-gather(bf16[1,256,512]{2,1,0:T(8,128)(2,1)} %param.16), channel_id=1, replica_groups=mesh['ctx'=2,'hs'=16] {'ctx'}, dimensions={1}, use_global_device_ids=true | all-gather | bytes 786432 | tf_op jit(solution)/shard_map/all_gather | solution.py:43
  15.6 7.2 %all_gather.23 = bf16[1,512,512]{2,1,0:T(8,128)(2,1)S(1)} all-gather(bf16[1,256,512]{2,1,0:T(8,128)(2,1)} %param.14), channel_id=1, replica_groups=mesh['ctx'=2,'hs'=16] {'ctx'}, dimensions={1}, use_global_device_ids=true | all-gather | bytes 786432 | tf_op jit(solution)/shard_map/all_gather | solution.py:41
  22.8 6.1 %all_gather.22 = bf16[1,512,512]{2,1,0:T(8,128)(2,1)S(1)} all-gather(bf16[1,256,512]{2,1,0:T(8,128)(2,1)} %param.15), channel_id=1, replica_groups=mesh['ctx'=2,'hs'=16] {'ctx'}, dimensions={1}, use_global_device_ids=true | all-gather | bytes 786432 | tf_op jit(solution)/shard_map/all_gather | solution.py:42
  30.8 1.8 %fusion.33 = f32[512,512]{1,0:T(8,128)} fusion(bf16[1,512,512]{2,1,0:T(8,128)(2,1)S(1)} %copy-done, f32[512,512]{1,0:T(8,128)S(1)} %fusion.28, f32[512,512]{1,0:T(8,128)S(1)} %fusion.23, f32[512,512]{1,0:T(8,128)S(1)} %fusion.30), kind=kOutput, calls=%fused_computation.50 | convolution fusion | flops 271056896 | bytes 4718592 | tf_op jit(solution)/shard_map/dot_general | solution.py:19
  32.6 1.5 fusion.19
  34.3 2.9 %fusion.20 = f32[512,512]{1,0:T(8,128)} fusion(f32[512,512]{1,0:T(8,128)} %copy-done.4, bf16[1,512,512]{2,1,0:T(8,128)(2,1)S(1)} %copy-done.5, f32[512]{0:T(512)S(1)} %bitcast.78, f32[512,512]{1,0:T(8,128)S(1)} %fusion.28), kind=kOutput, calls=%fused_computation.40 | convolution fusion | flops 270794752 | bytes 3672064 | tf_op jit(solution)/shard_map/dot_general | solution.py:19
  37.8 19.2 %reduce-scatter.4.cloned.1.call-done = f32[256,512]{1,0:T(8,128)} async-done(((f32[512,512]{1,0:T(8,128)}), f32[256,512]{1,0:T(8,128)}) %reduce-scatter.4.cloned.1.call-update) | async-done | bytes 524304 | tf_op jit(solution)/shard_map/reduce_scatter | solution.py:63
  57.0 1.2 fusion.16
  58.2 1.1 multiply_convert_fusion.7
  59.4 7.7 %all_gather.24 = bf16[512,512]{1,0:T(8,128)(2,1)S(1)} all-gather(bf16[256,512]{1,0:T(8,128)(2,1)S(1)} %multiply_convert_fusion.7), channel_id=1, replica_groups=mesh['ctx'=2,'hs'=16] {'ctx'}, dimensions={0}, use_global_device_ids=true | all-gather | bytes 786432 | tf_op jit(solution)/shard_map/all_gather | solution.py:71
  67.1 13.5 %reduce-scatter.6.cloned.1.call-done = f32[256,512]{1,0:T(8,128)} async-done(((f32[512,512]{1,0:T(8,128)}), f32[256,512]{1,0:T(8,128)}) %reduce-scatter.6.cloned.1.call-update) | async-done | bytes 524304 | tf_op jit(solution)/shard_map/reduce_scatter | solution.py:64
  80.6 1.2 fusion.17
  81.9 1.1 multiply_convert_fusion.6
  83.0 8.0 %all_gather.25 = bf16[512,512]{1,0:T(8,128)(2,1)S(1)} all-gather(bf16[256,512]{1,0:T(8,128)(2,1)S(1)} %multiply_convert_fusion.6), channel_id=1, replica_groups=mesh['ctx'=2,'hs'=16] {'ctx'}, dimensions={0}, use_global_device_ids=true | all-gather | bytes 786432 | tf_op jit(solution)/shard_map/all_gather | solution.py:72
  91.0 13.2 %reduce-scatter.8.cloned.1.call-done = f32[256,512]{1,0:T(8,128)} async-done(((f32[512,512]{1,0:T(8,128)}), f32[256,512]{1,0:T(8,128)}) %reduce-scatter.8.cloned.1.call-update) | async-done | bytes 524304 | tf_op jit(solution)/shard_map/reduce_scatter | solution.py:65
  104.2 1.2 fusion.18
  106.6 8.0 %all_gather.26 = bf16[512,512]{1,0:T(8,128)(2,1)} all-gather(bf16[256,512]{1,0:T(8,128)(2,1)S(1)} %multiply_convert_fusion.5), channel_id=1, replica_groups=mesh['ctx'=2,'hs'=16] {'ctx'}, dimensions={0}, use_global_device_ids=true | all-gather | bytes 786432 | tf_op jit(solution)/shard_map/all_gather | solution.py:73
  114.6 1.5 convolution_bitcast_fusion.1
  116.1 2.0 %convolution_convert_fusion = bf16[512,512]{1,0:T(8,128)(2,1)S(1)} fusion(bf16[512,512]{1,0:T(8,128)(2,1)} %all_gather.26, bf16[512,512]{1,0:T(8,128)(2,1)S(1)} %all_gather.25, f32[512,512]{1,0:T(8,128)S(1)} %convolution_bitcast_fusion.1, bf16[1,512,512]{2,1,0:T(8,128)(2,1)} %param.12), kind=kOutput, calls=%fused_computation.9 | convolution fusion | flops 538705920 | bytes 3145728 | tf_op jit(solution)/shard_map/dot_general | solution.py:78
  118.1 20.5 %all_to_all.4 = bf16[16,32,512]{2,1,0:T(8,128)(2,1)S(1)} all-to-all(bf16[16,32,512]{2,1,0:T(8,128)(2,1)S(1)} %bitcast.75), channel_id=1, replica_groups=mesh['ctx'=2,'hs'=16] {'hs'}, dimensions={0} | all-to-all | bytes 1048576 | tf_op jit(solution)/shard_map/all_to_all | solution.py:85
  140.3 1.2 mul.142
  141.5 2.1 %mul.143 = f32[32,4,2048]{2,1,0:T(4,128)S(1)} reshape(f32[32,4,4,512]{3,2,1,0:T(4,128)} %mul.142) | data formatting | bytes 2097152 | tf_op jit(solution)/shard_map/mul | solution.py:91
  143.6 1.7 %fusion.15 = bf16[32,4,2048]{2,1,0:T(4,128)(2,1)S(1)} fusion(bf16[32,4,2048]{2,1,0:T(4,128)(2,1)} %param.18, f32[32,4,2048]{2,1,0:T(4,128)S(1)} %reshape.117, f32[32,4,2048]{2,1,0:T(4,128)S(1)} %mul.143, f32[2048]{0:T(1024)S(1)} %copy-done.6), kind=kLoop, calls=%fused_computation.29 | loop fusion | flops 2359296 | bytes 3153920 | tf_op jit(solution)/shard_map/convert_element_type | solution.py:95
  145.5 2.9 %convolution_convert_fusion.1 = bf16[128,1024]{1,0:T(8,128)(2,1)S(1)} fusion(bf16[128,2048]{1,0:T(8,128)(2,1)S(1)} %reshape.111, bf16[2048,1024]{1,0:T(8,128)(2,1)} %all-gather.2.cloned.1.call-done), kind=kOutput, calls=%fused_computation.11 | convolution fusion | flops 537001984 | bytes 4980736 | tf_op jit(solution)/shard_map/dot_general | solution.py:99
  (40 shorter events, 6.4 us)
Async XLA Ops:
  7.4 21.5 %copy-start = (bf16[1,512,512]{2,1,0:T(8,128)(2,1)S(1)}, bf16[1,512,512]{2,1,0:T(8,128)(2,1)}, u32[]{:S(2)}) copy-start(bf16[1,512,512]{2,1,0:T(8,128)(2,1)} %param.10) | copy-start | bytes 1572868
  7.4 22.4 %copy-start.7 = (f32[1,512]{1,0:T(1,128)S(1)}, f32[1,512]{1,0:T(1,128)}, u32[]{:S(2)}) copy-start(f32[1,512]{1,0:T(1,128)} %param.13) | copy-start | bytes 6148
  7.4 22.5 %copy-start.5 = (bf16[1,512,512]{2,1,0:T(8,128)(2,1)S(1)}, bf16[1,512,512]{2,1,0:T(8,128)(2,1)}, u32[]{:S(2)}) copy-start(bf16[1,512,512]{2,1,0:T(8,128)(2,1)} %param.11) | copy-start | bytes 1572868
  7.4 49.6 %reduce-scatter.4.cloned.1.call-start = ((), (), s32[]{:S(2)}) async-start(), calls=%async_computation.4 | async-start | bytes 1572864 | tf_op jit(solution)/shard_map/reduce_scatter | solution.py:63
  29.8 1.0 copy-start.4
  32.6 48.0 %reduce-scatter.6.cloned.1.call-start = ((), (), s32[]{:S(2)}) async-start(), calls=%async_computation.5 | async-start | bytes 1572864 | tf_op jit(solution)/shard_map/reduce_scatter | solution.py:64
  34.2 22.8 %copy-start.1 = (bf16[1,256,512]{2,1,0:T(8,128)(2,1)S(1)}, bf16[1,256,512]{2,1,0:T(8,128)(2,1)}, u32[]{:S(2)}) copy-start(bf16[1,256,512]{2,1,0:T(8,128)(2,1)} %param.14) | copy-start | bytes 786436
  34.2 46.4 %copy-start.2 = (bf16[1,256,512]{2,1,0:T(8,128)(2,1)S(1)}, bf16[1,256,512]{2,1,0:T(8,128)(2,1)}, u32[]{:S(2)}) copy-start(bf16[1,256,512]{2,1,0:T(8,128)(2,1)} %param.15) | copy-start | bytes 786436
  34.2 70.0 %reduce-scatter.8.cloned.1.call-start = ((), (), s32[]{:S(2)}) async-start(), calls=%async_computation.6 | async-start | bytes 1572864 | tf_op jit(solution)/shard_map/reduce_scatter | solution.py:65
  37.2 67.0 %copy-start.3 = (bf16[1,256,512]{2,1,0:T(8,128)(2,1)S(1)}, bf16[1,256,512]{2,1,0:T(8,128)(2,1)}, u32[]{:S(2)}) copy-start(bf16[1,256,512]{2,1,0:T(8,128)(2,1)} %param.16) | copy-start | bytes 786436
  37.2 108.3 %all-gather.2.cloned.1.call-start = ((), (), s32[]{:S(2)}) async-start(), calls=%async_computation.7 | async-start | bytes 4456448 | tf_op jit(solution)/shard_map/all_gather | solution.py:98
  138.7 4.9 %copy-start.6 = (f32[2048]{0:T(1024)S(1)}, f32[2048]{0:T(1024)}, u32[]{:S(2)}) copy-start(f32[2048]{0:T(1024)} %param.17) | copy-start | bytes 24580
Sparse Core Ops, SparseCore 0:
  32.7 24.2 reduce-scatter.3
  59.2 21.3 reduce-scatter.5
  82.9 21.3 reduce-scatter.7
Sparse Core Ops, SparseCore 1:
  39.9 53.8 all-gather.1
where the time goes:
time: 159 us; the launch traced here: 156 us
  blocking collectives  65.7 us (41%)
  waiting for transfers between devices  46.5 us (29%)
  between operations  14.8 us (9%)
  matrix products  14.1 us (9%)
  other arithmetic  9.17 us (6%)
  local copies, waits for them, and re-layouts  6.1 us (4%)
    all_to_all x1, blocking collectives, body(): lax.all_to_all(blocks, 'hs', split_axis=0, concat_axis=2, tiled=True)  20.5 us
    reduce_scatter x1, waiting for transfers between devices, body(): lax.psum_scatter(grad_gate, 'ctx', scatter_dimension=0, tiled=True)  19.2 us
    reduce_scatter x1, waiting for transfers between devices, body(): lax.psum_scatter(grad_up, 'ctx', scatter_dimension=0, tiled=True)  13.5 us
    reduce_scatter x1, waiting for transfers between devices, body(): lax.psum_scatter(grad_down, 'ctx', scatter_dimension=0, tiled=True)  13.2 us
    all_gather x1, blocking collectives, body(): lax.all_gather(fast_down, 'ctx', axis=1, tiled=True)  8.19 us
    all_gather x1, blocking collectives, body(): lax.all_gather(part_up, 'ctx', axis=0, tiled=True)  8.03 us
    all_gather x1, blocking collectives, body(): lax.all_gather(part_down, 'ctx', axis=0, tiled=True)  8 us
    all_gather x1, blocking collectives, body(): lax.all_gather(part_gate, 'ctx', axis=0, tiled=True)  7.7 us
  transfers between devices with their start and end apart: 4, of which 3 were waited for; matrix products, arithmetic and copies ran while one was open for 14% of the time, Pallas kernels for 0%

commit v1 on v0

--- a/solution.py
+++ b/solution.py
@@ -1,6 +1,10 @@
+import functools
+
 import jax
 import jax.numpy as jnp
 from jax import lax
+from jax.experimental import pallas as pl
+from jax.experimental.pallas import tpu as pltpu
 from jax.sharding import PartitionSpec as P
 
 epsilon = 1e-06
@@ -100,9 +104,325 @@
     return result.astype(jnp.bfloat16).reshape(token_count, seq_count, out_cols)
 
 
+MESH = pl.DeviceIdType.MESH
+
+
+def inner_cols(left, right):
+    return lax.dot_general(
+        left, right, (((1,), (1,)), ((), ())), preferred_element_type=jnp.float32
+    )
+
+
+def layer_kernel(
+    layers,
+    pieces,
+    gate_hbm,
+    up_hbm,
+    down_hbm,
+    key_hbm,
+    scaled_hbm,
+    query_hbm,
+    side_hbm,
+    weight_hbm,
+    gain_ref,
+    out_ref,
+    fast,
+    fresh,
+    keys,
+    scaled,
+    queries,
+    side,
+    full,
+    grads,
+    heads,
+    mixed,
+    normed,
+    local_sem,
+    ctx_send,
+    ctx_recv,
+    full_send,
+    full_recv,
+    head_send,
+    head_recv,
+):
+    ctx = lax.axis_index("ctx")
+    me = lax.axis_index("hs")
+    other = 1 - ctx
+    count = 4 * layers
+    depth, inner = me // 4, me % 4
+    row, core = inner // 2, inner % 2
+    row_peer = depth * 4 + (1 - row) * 2 + core
+    core_peer = depth * 4 + row * 2 + (1 - core)
+
+    def remote(source, target, send, recv, device):
+        return pltpu.make_async_remote_copy(
+            src_ref=source,
+            dst_ref=target,
+            send_sem=send,
+            recv_sem=recv,
+            device_id=device,
+            device_id_type=MESH,
+        )
+
+    part = gate_hbm.shape[1]
+    tokens = key_hbm.shape[1]
+    piece = tokens // pieces
+    shard = weight_hbm.shape[0]
+
+    def rows(start, size):
+        return pl.ds(pl.multiple_of(start, size), size)
+
+    weights = (gate_hbm, up_hbm, down_hbm)
+    local = []
+    for i, source in enumerate(weights):
+        local.append(
+            pltpu.make_async_copy(source.at[0], fast.at[i, rows(ctx * part, part)], local_sem.at[i])
+        )
+    local.append(
+        pltpu.make_async_copy(key_hbm.at[0], keys.at[rows(ctx * tokens, tokens)], local_sem.at[3])
+    )
+    local.append(
+        pltpu.make_async_copy(scaled_hbm, scaled.at[rows(ctx * tokens, tokens)], local_sem.at[4])
+    )
+    local.append(pltpu.make_async_copy(weight_hbm, full.at[rows(me * shard, shard)], local_sem.at[5]))
+    local.append(pltpu.make_async_copy(query_hbm.at[0], queries, local_sem.at[6]))
+    local.append(pltpu.make_async_copy(side_hbm, side, local_sem.at[7]))
+    for copy in local:
+        copy.start()
+
+    barrier = pltpu.get_barrier_semaphore()
+    pl.semaphore_signal(barrier, inc=1, device_id={"ctx": other}, device_id_type=MESH)
+    for step in range(1, count):
+        pl.semaphore_signal(
+            barrier, inc=1, device_id={"hs": (me + step) % count}, device_id_type=MESH
+        )
+    pl.semaphore_wait(barrier, count)
+
+    swaps = []
+    for i, source in enumerate(weights):
+        swaps.append((source.at[0], lambda who, i=i: fast.at[i, rows(who * part, part)]))
+    for j in range(pieces):
+        for source, target in ((key_hbm.at[0], keys), (scaled_hbm, scaled)):
+            swaps.append(
+                (
+                    source.at[pl.ds(j * piece, piece)],
+                    lambda who, target=target, j=j: target.at[
+                        rows(who * tokens + j * piece, piece)
+                    ],
+                )
+            )
+    outgoing = [
+        remote(source, target(ctx), ctx_send.at[i], ctx_recv.at[i], {"ctx": other})
+        for i, (source, target) in enumerate(swaps)
+    ]
+    incoming = [
+        remote(source, target(other), ctx_send.at[i], ctx_recv.at[i], {"ctx": other})
+        for i, (source, target) in enumerate(swaps)
+    ]
+    for copy in outgoing:
+        copy.start()
+
+    sent = []
+
+    def forward(source, index, device):
+        slot = full_send.at[len(sent)]
+        copy = remote(
+            source, full.at[rows(index * shard, shard)], slot, full_recv.at[index], {"hs": device}
+        )
+        copy.start()
+        sent.append(copy)
+
+    def arrived(index):
+        block = full.at[rows(index * shard, shard)]
+        remote(block, block, full_send.at[0], full_recv.at[index], {"hs": core_peer}).wait_recv()
+        return block
+
+    for step in range(1, layers):
+        forward(weight_hbm, me, ((depth + step) % layers) * 4 + inner)
+    forward(weight_hbm, me, row_peer)
+    forward(weight_hbm, me, core_peer)
+
+    def learn(start, first):
+        key_part = keys[rows(start, piece), :]
+        scaled_part = scaled[rows(start, piece), :]
+        pre_gate = inner_cols(key_part, fast[0])
+        pre_up = inner_cols(key_part, fast[1])
+        sig_gate = jax.nn.sigmoid(pre_gate)
+        act_gate = pre_gate * sig_gate
+        hidden = (act_gate * pre_up).astype(jnp.bfloat16)
+        back_hidden = jnp.dot(scaled_part, fast[2], preferred_element_type=jnp.float32)
+        back_gate = (
+            back_hidden * pre_up * sig_gate * (1.0 + pre_gate * (1.0 - sig_gate))
+        ).astype(jnp.bfloat16)
+        back_up = (back_hidden * act_gate).astype(jnp.bfloat16)
+        terms = (
+            inner_rows(back_gate, key_part),
+            inner_rows(back_up, key_part),
+            inner_rows(scaled_part, hidden),
+        )
+        for i, term in enumerate(terms):
+            grads[i] = term if first else grads[i] + term
+
+    for copy in local[:5]:
+        copy.wait()
+    for copy in incoming[:3]:
+        copy.wait_recv()
+    for j in range(pieces):
+        learn(ctx * tokens + j * piece, j == 0)
+
+    for step in range(1, layers):
+        index = ((depth + layers - step) % layers) * 4 + inner
+        block = arrived(index)
+        forward(block, index, row_peer)
+        forward(block, index, core_peer)
+
+    for j in range(pieces):
+        if j == pieces - 1:
+            for step in range(layers):
+                index = ((depth + layers - step) % layers) * 4 + (1 - row) * 2 + core
+                forward(arrived(index), index, core_peer)
+        incoming[3 + 2 * j].wait_recv()
+        incoming[4 + 2 * j].wait_recv()
+        learn(other * tokens + j * piece, False)
+
+    for i in range(3):
+        fresh[i] = rescale_rows(fast[i], grads[i])
+
+    local[6].wait()
+    block_rows = tokens // count
+    step_rows = 4 * block_rows
+    copies = []
+    for step in range(1, layers + 1):
+        target = (depth + step) % layers
+        query_part = queries[rows(target * step_rows, step_rows), :]
+        query_gate = inner_cols(query_part, fresh[0])
+        query_up = inner_cols(query_part, fresh[1])
+        query_hidden = (query_gate * jax.nn.sigmoid(query_gate) * query_up).astype(jnp.bfloat16)
+        head_part = inner_cols(query_hidden, fresh[2]).astype(jnp.bfloat16)
+        heads[rows(target * step_rows, step_rows), :] = head_part
+        for i in range(4):
+            device = target * 4 + (inner + i) % 4
+            source = heads.at[rows(device * block_rows, block_rows)]
+            if step == layers and i == 0:
+                mixed[me] = source[...]
+            else:
+                slot = len(copies)
+                copy = remote(
+                    source, mixed.at[me], head_send.at[slot], head_recv.at[me], {"hs": device}
+                )
+                copy.start()
+                copies.append(copy)
+
+    for copy in (local[5], local[7]):
+        copy.wait()
+    for step in range(layers):
+        for other_row in range(2):
+            arrived(((depth + step) % layers) * 4 + ((row + other_row) % 2) * 2 + (1 - core))
+    for copy in outgoing + sent:
+        copy.wait_send()
+    for step in range(1, count):
+        index = (me + step) % count
+        remote(
+            heads.at[pl.ds(0, block_rows)],
+            mixed.at[index],
+            head_send.at[0],
+            head_recv.at[index],
+            {"hs": core_peer},
+        ).wait_recv()
+    for copy in copies:
+        copy.wait_send()
+
+    size = mixed.shape[2]
+    head_count = side.shape[2] // size
+    for seq in range(side.shape[0]):
+        for head in range(head_count):
+            columns = slice(head * size, (head + 1) * size)
+            value = mixed[seq * head_count + head].astype(jnp.float32)
+            square = jnp.mean(value * value, -1, keepdims=True)
+            value = value * lax.rsqrt(square + epsilon) * gain_ref[:, columns]
+            gate = side[seq, :, columns].astype(jnp.float32)
+            normed[seq * block_rows : (seq + 1) * block_rows, columns] = (
+                value * (gate * jax.nn.sigmoid(gate))
+            ).astype(jnp.bfloat16)
+    result = jnp.dot(normed[...], full[...], preferred_element_type=jnp.float32)
+    for seq in range(side.shape[0]):
+        out_ref[seq] = result[seq * block_rows : (seq + 1) * block_rows].astype(jnp.bfloat16)
+
+
+def swapped_body(
+    key_rows,
+    value_rows,
+    query_rows,
+    step_rates,
+    fast_gate,
+    fast_up,
+    fast_down,
+    out_gain,
+    gate_input,
+    out_weight,
+):
+    layers = lax.axis_size("hs") // 4
+    count = 4 * layers
+    pieces = 2
+    tokens, size = key_rows.shape[1:]
+    hidden_size = 2 * fast_gate.shape[1]
+    block_rows, seq_count, width = gate_input.shape
+    columns = out_weight.shape[1]
+    scaled = (step_rates[0][:, None] * value_rows[0].astype(jnp.float32)).astype(jnp.bfloat16)
+    side = gate_input.transpose(1, 0, 2)
+    anywhere = pl.BlockSpec(memory_space=pl.ANY)
+    inside = pl.BlockSpec(memory_space=pltpu.VMEM)
+    half = jnp.bfloat16
+    result = pl.pallas_call(
+        functools.partial(layer_kernel, layers, pieces),
+        out_shape=jax.ShapeDtypeStruct((seq_count, block_rows, columns), half),
+        in_specs=[anywhere] * 8 + [inside],
+        out_specs=inside,
+        scratch_shapes=[
+            pltpu.VMEM((3, hidden_size, size), half),
+            pltpu.VMEM((3, hidden_size, size), half),
+            pltpu.VMEM((2 * tokens, size), half),
+            pltpu.VMEM((2 * tokens, size), half),
+            pltpu.VMEM((tokens, size), half),
+            pltpu.VMEM((seq_count, block_rows, width), half),
+            pltpu.VMEM((width, columns), half),
+            pltpu.VMEM((3, hidden_size, size), jnp.float32),
+            pltpu.VMEM((tokens, size), half),
+            pltpu.VMEM((count, block_rows, size), half),
+            pltpu.VMEM((seq_count * block_rows, width), half),
+            pltpu.SemaphoreType.DMA((8,)),
+            pltpu.SemaphoreType.DMA((3 + 2 * pieces,)),
+            pltpu.SemaphoreType.DMA((3 + 2 * pieces,)),
+            pltpu.SemaphoreType.DMA((4 * layers,)),
+            pltpu.SemaphoreType.DMA((count,)),
+            pltpu.SemaphoreType.DMA((count,)),
+            pltpu.SemaphoreType.DMA((count,)),
+        ],
+        compiler_params=pltpu.CompilerParams(
+            collective_id=0, has_side_effects=True, vmem_limit_bytes=60 * 1024 * 1024
+        ),
+    )(
+        fast_gate,
+        fast_up,
+        fast_down,
+        key_rows,
+        scaled,
+        query_rows,
+        side,
+        out_weight,
+        out_gain[None],
+    )
+    return result.transpose(1, 0, 2)
+
+
 def solution(mesh):
+    def step(*arrays):
+        paired = mesh.shape["ctx"] == 2 and mesh.shape["hs"] % 4 == 0
+        paired = paired and arrays[0].shape[0] == 1
+        return (swapped_body if paired else body)(*arrays)
+
     return jax.shard_map(
-        body,
+        step,
         mesh=mesh,
         in_specs=(
             P("hs", "ctx", None),

time: 159 us -> 69.6 us (0.44); the launches traced: 156 us -> 69.4 us
  blocking collectives: 65.7 us -> 0 us
  Pallas kernels: 0 us -> 63.7 us
  waiting for transfers between devices: 46.5 us -> 0 us
  between operations: 14.8 us -> 0.01 us
  matrix products: 14.1 us -> 0 us
  other arithmetic: 9.17 us -> 2.04 us
  local copies, waits for them, and re-layouts: 6.1 us -> 3.62 us
    pallas_call x0 -> x1, Pallas kernels: none -> 63.7 us  [swapped_body(): pl.pallas_call(functools.partial(layer_kernel, layers, pieces), out_shape...]
    reduce_scatter x3 -> x0, waiting for transfers between devices: 45.9 us -> none  [the longest x1 19.2 us: body(): lax.psum_scatter(grad_gate, 'ctx', scatter_dimension=0, tiled=True)]
    all_gather x6 -> x0, blocking collectives: 45.2 us -> none  [the longest x1 8.19 us: body(): lax.all_gather(fast_down, 'ctx', axis=1, tiled=True)]
    all_to_all x1 -> x0, blocking collectives: 20.5 us -> none  [body(): lax.all_to_all(blocks, 'hs', split_axis=0, concat_axis=2, tiled=True)]
    dot_general x9 -> x0, matrix products: 14.1 us -> none  [the longest x3 6.24 us: inner_rows(): lax.dot_general(left, right, (((0,), (0,)), ((), ())), preferred_element_...]
    reduce_sum x4 -> x0, other arithmetic: 3.84 us -> none  [the longest x3 3.67 us: rescale_rows(): jnp.mean(base * base, -1, keepdims=True) + epsilon]
    mul x2 -> x0, local copies, waits for them, and re-layouts: 3.29 us -> none  [body(): mixed * lax.rsqrt(square + epsilon)]
    convert_element_type x5 -> x1, other arithmetic: 5.29 us -> 2.04 us  [swapped_body(): (step_rates[0][:, None] * value_rows[0].astype(jnp.float32)).astype(jnp.b...]
  transfers between devices with their start and end apart: 4 -> 0, of which waited for: 3 -> 0; matrix products, arithmetic and copies ran while one was open for 14% -> 0% of each run, Pallas kernels for 0% -> 0%
where the time goes in v1:
time: 69.6 us; the launch traced here: 69.4 us
  Pallas kernels  63.7 us (92%)
  local copies, waits for them, and re-layouts  3.62 us (5%)
  other arithmetic  2.04 us (3%)
    pallas_call x1, Pallas kernels, swapped_body(): pl.pallas_call(functools.partial(layer_kernel, layers, pieces), out_shape...  63.7 us
    convert_element_type x1, other arithmetic, swapped_body(): (step_rates[0][:, None] * value_rows[0].astype(jnp.float32)).astype(jnp.b...  2.04 us
    transpose x1, local copies, waits for them, and re-layouts, swapped_body(): return result.transpose(1, 0, 2)  1.86 us
    unnamed x5, local copies, waits for them, and re-layouts  1.77 us

profile of v1, /device:TPU:13, one launch (start us, length us, event | category | flops | bytes accessed | tf_op | source)
XLA Modules:
  0.0 69.4 jit_solution(10535072746930028673)
XLA Ops:
  0.0 0.0 copy-start.1
  0.0 0.7 copy-done.1
  0.7 0.0 copy-start
  0.7 2.0 %fusion.scaled_hbm = bf16[512,512]{1,0:T(8,128)(2,1)} fusion(bf16[1,512,512]{2,1,0:T(8,128)(2,1)} %param.11, f32[512]{0:T(512)S(1)} %bitcast.12), kind=kLoop, calls=%fused_computation.1 | loop fusion | flops 786432 | bytes 1050624 | tf_op jit(solution)/shard_map/convert_element_type | solution.py:371
  2.7 0.0 copy-done
  2.7 1.1 %copy.14 = bf16[32,4,2048]{2,0,1:T(8,128)(2,1)} copy(bf16[32,4,2048]{2,1,0:T(4,128)(2,1)S(1)} %copy-done) | data formatting | bytes 1048576 | tf_op args[8]
  3.8 63.7 %shard_map.100 = bf16[4,32,1024]{2,1,0:T(8,128)(2,1)} custom-call(bf16[1,256,512]{2,1,0:T(8,128)(2,1)} %gate_hbm.1, bf16[1,256,512]{2,1,0:T(8,128)(2,1)} %up_hbm.1, bf16[1,256,512]{2,1,0:T(8,128)(2,1)} %down_hbm.1, bf16[1,512,512]{2,1,0:T(8,128)(2,1)} %key_hbm.1, bf16[512,512]{1,0:T(8,128)(2,1)} %fusion.scaled_hbm, bf16[1,512,512]{2,1,0:T(8,128)(2,1)} %query_hbm.1, ...), custom_call_target="tpu_custom_call" | custom-call | tf_op jit(solution)/shard_map/pallas_call | solution.py:376
  67.6 1.9 %copy.12 = bf16[32,4,1024]{2,1,0:T(4,128)(2,1)} copy(bf16[32,4,1024]{2,0,1:T(8,128)(2,1)} %bitcast.10) | data formatting | bytes 524288 | tf_op jit(solution)/shard_map/transpose | solution.py:415
Async XLA Ops:
  0.0 0.7 copy-start.1
  0.7 2.0 %copy-start = (bf16[32,4,2048]{2,1,0:T(4,128)(2,1)S(1)}, bf16[32,4,2048]{2,1,0:T(4,128)(2,1)}, u32[]{:S(2)}) copy-start(bf16[32,4,2048]{2,1,0:T(4,128)(2,1)} %param.18) | copy-start | bytes 1572868

commit v2 on v1

--- a/solution.py
+++ b/solution.py
@@ -144,6 +144,8 @@
     full_recv,
     head_send,
     head_recv,
+    fresh_send,
+    fresh_recv,
 ):
     ctx = lax.axis_index("ctx")
     me = lax.axis_index("hs")
@@ -153,6 +155,9 @@
     row, core = inner // 2, inner % 2
     row_peer = depth * 4 + (1 - row) * 2 + core
     core_peer = depth * 4 + row * 2 + (1 - core)
+    pair = depth * 4 + row * 2 + ctx
+    owner = core == ctx
+    helper = core != ctx
 
     def remote(source, target, send, recv, device):
         return pltpu.make_async_remote_copy(
@@ -187,16 +192,26 @@
     local.append(pltpu.make_async_copy(weight_hbm, full.at[rows(me * shard, shard)], local_sem.at[5]))
     local.append(pltpu.make_async_copy(query_hbm.at[0], queries, local_sem.at[6]))
     local.append(pltpu.make_async_copy(side_hbm, side, local_sem.at[7]))
-    for copy in local:
-        copy.start()
+    owned = [0, 1, 2, 3, 4, 6]
+    for i in (5, 7):
+        local[i].start()
+
+    @pl.when(owner)
+    def _():
+        for i in owned:
+            local[i].start()
 
     barrier = pltpu.get_barrier_semaphore()
     pl.semaphore_signal(barrier, inc=1, device_id={"ctx": other}, device_id_type=MESH)
     for step in range(1, count):
-        pl.semaphore_signal(
-            barrier, inc=1, device_id={"hs": (me + step) % count}, device_id_type=MESH
-        )
-    pl.semaphore_wait(barrier, count)
+        for side_ctx in (ctx, other):
+            pl.semaphore_signal(
+                barrier,
+                inc=1,
+                device_id={"ctx": side_ctx, "hs": (me + step) % count},
+                device_id_type=MESH,
+            )
+    pl.semaphore_wait(barrier, 2 * count - 1)
 
     swaps = []
     for i, source in enumerate(weights):
@@ -219,28 +234,82 @@
         remote(source, target(other), ctx_send.at[i], ctx_recv.at[i], {"ctx": other})
         for i, (source, target) in enumerate(swaps)
     ]
-    for copy in outgoing:
-        copy.start()
-
-    sent = []
-
-    def forward(source, index, device):
-        slot = full_send.at[len(sent)]
-        copy = remote(
-            source, full.at[rows(index * shard, shard)], slot, full_recv.at[index], {"hs": device}
+    asked = remote(
+        query_hbm.at[0],
+        queries,
+        ctx_send.at[len(swaps)],
+        ctx_recv.at[len(swaps)],
+        {"ctx": other, "hs": core_peer},
+    )
+
+    @pl.when(helper)
+    def _():
+        for copy in outgoing:
+            copy.start()
+        asked.start()
+
+    def full_copy(source, index, slot, device):
+        return remote(
+            source,
+            full.at[rows(index * shard, shard)],
+            full_send.at[slot],
+            full_recv.at[index],
+            {"hs": device},
         )
-        copy.start()
-        sent.append(copy)
 
     def arrived(index):
         block = full.at[rows(index * shard, shard)]
         remote(block, block, full_send.at[0], full_recv.at[index], {"hs": core_peer}).wait_recv()
-        return block
-
-    for step in range(1, layers):
-        forward(weight_hbm, me, ((depth + step) % layers) * 4 + inner)
-    forward(weight_hbm, me, row_peer)
-    forward(weight_hbm, me, core_peer)
+
+    def held(index):
+        return full.at[rows(index * shard, shard)]
+
+    sends = [
+        (depth < layers - 1, full_copy(weight_hbm, me, 0, me + 4)),
+        (depth > 0, full_copy(weight_hbm, me, 1, me - 4)),
+        (None, full_copy(weight_hbm, me, 2, row_peer)),
+        (None, full_copy(weight_hbm, me, 3, core_peer)),
+    ]
+
+    def guarded(condition, action):
+        if condition is None:
+            action()
+        else:
+            pl.when(condition)(action)
+
+    for condition, copy in sends:
+        guarded(condition, copy.start)
+
+    def relay(hop):
+        for turn, (exists, onward) in enumerate(
+            (
+                (depth >= hop, depth < layers - 1),
+                (depth + hop <= layers - 1, depth > 0),
+            )
+        ):
+            index = me - 4 * hop if turn == 0 else me + 4 * hop
+            slot = 4 + ((hop - 1) * 2 + turn) * 3
+            next_device = me + 4 if turn == 0 else me - 4
+            made = [
+                (exists & onward, full_copy(held(index), index, slot, next_device)),
+                (exists, full_copy(held(index), index, slot + 1, row_peer)),
+                (exists, full_copy(held(index), index, slot + 2, core_peer)),
+            ]
+            pl.when(exists)(functools.partial(arrived, index))
+            for condition, copy in made:
+                guarded(condition, copy.start)
+            sends.extend(made)
+
+    crossed = []
+    for step in range(layers):
+        index = ((depth + step) % layers) * 4 + (1 - row) * 2 + core
+        slot = 4 + 6 * (layers - 1) + step
+        crossed.append((index, full_copy(held(index), index, slot, core_peer)))
+
+    def cross():
+        for index, copy in crossed:
+            arrived(index)
+            copy.start()
 
     def learn(start, first):
         key_part = keys[rows(start, piece), :]
@@ -263,32 +332,50 @@
         for i, term in enumerate(terms):
             grads[i] = term if first else grads[i] + term
 
-    for copy in local[:5]:
-        copy.wait()
-    for copy in incoming[:3]:
-        copy.wait_recv()
+    handed = [
+        remote(fresh.at[i], fresh.at[i], fresh_send.at[i], fresh_recv.at[i], {"hs": core_peer})
+        for i in range(3)
+    ]
+    hops = list(range(1, layers))
+    if hops:
+        relay(hops.pop(0))
+
+    @pl.when(owner)
+    def _():
+        for i in owned[:5]:
+            local[i].wait()
+        for copy in incoming[:3]:
+            copy.wait_recv()
+        for j in range(pieces):
+            learn(ctx * tokens + j * piece, j == 0)
+
     for j in range(pieces):
-        learn(ctx * tokens + j * piece, j == 0)
-
-    for step in range(1, layers):
-        index = ((depth + layers - step) % layers) * 4 + inner
-        block = arrived(index)
-        forward(block, index, row_peer)
-        forward(block, index, core_peer)
-
-    for j in range(pieces):
-        if j == pieces - 1:
-            for step in range(layers):
-                index = ((depth + layers - step) % layers) * 4 + (1 - row) * 2 + core
-                forward(arrived(index), index, core_peer)
-        incoming[3 + 2 * j].wait_recv()
-        incoming[4 + 2 * j].wait_recv()
-        learn(other * tokens + j * piece, False)
-
-    for i in range(3):
-        fresh[i] = rescale_rows(fast[i], grads[i])
-
-    local[6].wait()
+        if hops:
+            relay(hops.pop(0))
+
+        @pl.when(owner)
+        def _():
+            incoming[3 + 2 * j].wait_recv()
+            incoming[4 + 2 * j].wait_recv()
+            learn(other * tokens + j * piece, False)
+
+    for hop in hops:
+        relay(hop)
+
+    @pl.when(owner)
+    def _():
+        for i in range(3):
+            fresh[i] = rescale_rows(fast[i], grads[i])
+            handed[i].start()
+        local[6].wait()
+
+    @pl.when(helper)
+    def _():
+        cross()
+        asked.wait_recv()
+        for copy in handed:
+            copy.wait_recv()
+
     block_rows = tokens // count
     step_rows = 4 * block_rows
     copies = []
@@ -303,25 +390,33 @@
         for i in range(4):
             device = target * 4 + (inner + i) % 4
             source = heads.at[rows(device * block_rows, block_rows)]
+            slot = len(copies)
+            copy = remote(
+                source,
+                mixed.at[pair],
+                head_send.at[slot],
+                head_recv.at[pair],
+                {"ctx": core, "hs": device},
+            )
+            condition = None
             if step == layers and i == 0:
-                mixed[me] = source[...]
-            else:
-                slot = len(copies)
-                copy = remote(
-                    source, mixed.at[me], head_send.at[slot], head_recv.at[me], {"hs": device}
-                )
-                copy.start()
-                copies.append(copy)
-
-    for copy in (local[5], local[7]):
-        copy.wait()
+                condition = helper
+
+                @pl.when(owner)
+                def _():
+                    mixed[me] = source[...]
+
+            guarded(condition, copy.start)
+            copies.append((condition, copy))
+
+    pl.when(owner)(cross)
+    for i in (5, 7):
+        local[i].wait()
     for step in range(layers):
         for other_row in range(2):
             arrived(((depth + step) % layers) * 4 + ((row + other_row) % 2) * 2 + (1 - core))
-    for copy in outgoing + sent:
-        copy.wait_send()
-    for step in range(1, count):
-        index = (me + step) % count
+
+    def head_arrived(index):
         remote(
             heads.at[pl.ds(0, block_rows)],
             mixed.at[index],
@@ -329,8 +424,26 @@
             head_recv.at[index],
             {"hs": core_peer},
         ).wait_recv()
-    for copy in copies:
+
+    for step in range(1, count):
+        head_arrived((me + step) % count)
+    pl.when(helper)(functools.partial(head_arrived, me))
+
+    for condition, copy in sends + copies:
+        guarded(condition, copy.wait_send)
+    for _, copy in crossed:
         copy.wait_send()
+
+    @pl.when(helper)
+    def _():
+        for copy in outgoing:
+            copy.wait_send()
+        asked.wait_send()
+
+    @pl.when(owner)
+    def _():
+        for copy in handed:
+            copy.wait_send()
 
     size = mixed.shape[2]
     head_count = side.shape[2] // size
@@ -391,12 +504,14 @@
             pltpu.VMEM((count, block_rows, size), half),
             pltpu.VMEM((seq_count * block_rows, width), half),
             pltpu.SemaphoreType.DMA((8,)),
-            pltpu.SemaphoreType.DMA((3 + 2 * pieces,)),
-            pltpu.SemaphoreType.DMA((3 + 2 * pieces,)),
-            pltpu.SemaphoreType.DMA((4 * layers,)),
+            pltpu.SemaphoreType.DMA((4 + 2 * pieces,)),
+            pltpu.SemaphoreType.DMA((4 + 2 * pieces,)),
+            pltpu.SemaphoreType.DMA((4 + 6 * (layers - 1) + layers,)),
             pltpu.SemaphoreType.DMA((count,)),
             pltpu.SemaphoreType.DMA((count,)),
             pltpu.SemaphoreType.DMA((count,)),
+            pltpu.SemaphoreType.DMA((3,)),
+            pltpu.SemaphoreType.DMA((3,)),
         ],
         compiler_params=pltpu.CompilerParams(
             collective_id=0, has_side_effects=True, vmem_limit_bytes=60 * 1024 * 1024

time: 69.6 us -> 53.2 us (0.76)
  Pallas kernels: 63.7 us -> 46.8 us
    pallas_call x1, Pallas kernels: 63.7 us -> 46.8 us  [swapped_body(): pl.pallas_call(functools.partial(layer_kernel, layers, pieces), out_shape...]
where the time goes in v2:
time: 53.2 us; the launch traced here: 52.4 us
  Pallas kernels  46.8 us (88%)
  local copies, waits for them, and re-layouts  3.62 us (7%)
  other arithmetic  2.04 us (4%)
    pallas_call x1, Pallas kernels, swapped_body(): pl.pallas_call(functools.partial(layer_kernel, layers, pieces), out_shape...  46.8 us
    convert_element_type x1, other arithmetic, swapped_body(): (step_rates[0][:, None] * value_rows[0].astype(jnp.float32)).astype(jnp.b...  2.04 us
    transpose x1, local copies, waits for them, and re-layouts, swapped_body(): return result.transpose(1, 0, 2)  1.86 us
    unnamed x5, local copies, waits for them, and re-layouts  1.77 us

profile of v2, /device:TPU:13, one launch (start us, length us, event | category | flops | bytes accessed | tf_op | source)
XLA Modules:
  0.0 52.4 jit_solution(12538174435976923711)
XLA Ops:
  0.0 0.0 copy-start.1
  0.0 0.7 %copy-done.1 = f32[1,512]{1,0:T(1,128)S(1)} copy-done((f32[1,512]{1,0:T(1,128)S(1)}, f32[1,512]{1,0:T(1,128)}, u32[]{:S(2)}) %copy-start.1) | copy-done | bytes 2072
  0.7 0.0 copy-start
  0.7 2.0 %fusion.scaled_hbm = bf16[512,512]{1,0:T(8,128)(2,1)} fusion(bf16[1,512,512]{2,1,0:T(8,128)(2,1)} %param.11, f32[512]{0:T(512)S(1)} %bitcast.12), kind=kLoop, calls=%fused_computation.1 | loop fusion | flops 786432 | bytes 1050624 | tf_op jit(solution)/shard_map/convert_element_type | solution.py:484
  2.7 0.0 copy-done
  2.7 1.1 %copy.14 = bf16[32,4,2048]{2,0,1:T(8,128)(2,1)} copy(bf16[32,4,2048]{2,1,0:T(4,128)(2,1)S(1)} %copy-done) | data formatting | bytes 1048576 | tf_op args[8]
  3.8 46.8 %shard_map.100 = bf16[4,32,1024]{2,1,0:T(8,128)(2,1)} custom-call(bf16[1,256,512]{2,1,0:T(8,128)(2,1)} %gate_hbm.1, bf16[1,256,512]{2,1,0:T(8,128)(2,1)} %up_hbm.1, bf16[1,256,512]{2,1,0:T(8,128)(2,1)} %down_hbm.1, bf16[1,512,512]{2,1,0:T(8,128)(2,1)} %key_hbm.1, bf16[512,512]{1,0:T(8,128)(2,1)} %fusion.scaled_hbm, bf16[1,512,512]{2,1,0:T(8,128)(2,1)} %query_hbm.1, ...), custom_call_target="tpu_custom_call" | custom-call | tf_op jit(solution)/shard_map/pallas_call | solution.py:489
  50.6 1.9 %copy.12 = bf16[32,4,1024]{2,1,0:T(4,128)(2,1)} copy(bf16[32,4,1024]{2,0,1:T(8,128)(2,1)} %bitcast.10) | data formatting | bytes 524288 | tf_op jit(solution)/shard_map/transpose | solution.py:530
Async XLA Ops:
  0.0 0.7 %copy-start.1 = (f32[1,512]{1,0:T(1,128)S(1)}, f32[1,512]{1,0:T(1,128)}, u32[]{:S(2)}) copy-start(f32[1,512]{1,0:T(1,128)} %param.13) | copy-start | bytes 6148
  0.7 2.0 %copy-start = (bf16[32,4,2048]{2,1,0:T(4,128)(2,1)S(1)}, bf16[32,4,2048]{2,1,0:T(4,128)(2,1)}, u32[]{:S(2)}) copy-start(bf16[32,4,2048]{2,1,0:T(4,128)(2,1)} %param.18) | copy-start | bytes 1572868

commit v3 on v2

--- a/solution.py
+++ b/solution.py
@@ -120,23 +120,27 @@
     up_hbm,
     down_hbm,
     key_hbm,
-    scaled_hbm,
+    value_hbm,
     query_hbm,
     side_hbm,
     weight_hbm,
+    rate_ref,
     gain_ref,
     out_ref,
     fast,
     fresh,
     keys,
-    scaled,
+    values,
+    rates,
     queries,
     side,
+    opened,
     full,
     grads,
     heads,
     mixed,
     normed,
+    laid,
     local_sem,
     ctx_send,
     ctx_recv,
@@ -187,7 +191,7 @@
         pltpu.make_async_copy(key_hbm.at[0], keys.at[rows(ctx * tokens, tokens)], local_sem.at[3])
     )
     local.append(
-        pltpu.make_async_copy(scaled_hbm, scaled.at[rows(ctx * tokens, tokens)], local_sem.at[4])
+        pltpu.make_async_copy(value_hbm.at[0], values.at[rows(ctx * tokens, tokens)], local_sem.at[4])
     )
     local.append(pltpu.make_async_copy(weight_hbm, full.at[rows(me * shard, shard)], local_sem.at[5]))
     local.append(pltpu.make_async_copy(query_hbm.at[0], queries, local_sem.at[6]))
@@ -217,7 +221,7 @@
     for i, source in enumerate(weights):
         swaps.append((source.at[0], lambda who, i=i: fast.at[i, rows(who * part, part)]))
     for j in range(pieces):
-        for source, target in ((key_hbm.at[0], keys), (scaled_hbm, scaled)):
+        for source, target in ((key_hbm.at[0], keys), (value_hbm.at[0], values)):
             swaps.append(
                 (
                     source.at[pl.ds(j * piece, piece)],
@@ -226,6 +230,7 @@
                     ],
                 )
             )
+    swaps.append((rate_ref, lambda who: rates))
     outgoing = [
         remote(source, target(ctx), ctx_send.at[i], ctx_recv.at[i], {"ctx": other})
         for i, (source, target) in enumerate(swaps)
@@ -244,7 +249,7 @@
 
     @pl.when(helper)
     def _():
-        for copy in outgoing:
+        for copy in outgoing[-1:] + outgoing[:-1]:
             copy.start()
         asked.start()
 
@@ -311,9 +316,12 @@
             arrived(index)
             copy.start()
 
-    def learn(start, first):
+    def learn(start, rate, first):
         key_part = keys[rows(start, piece), :]
-        scaled_part = scaled[rows(start, piece), :]
+        rate_column = jnp.broadcast_to(rate, (128, piece)).T[:, :1]
+        scaled_part = (rate_column * values[rows(start, piece), :].astype(jnp.float32)).astype(
+            jnp.bfloat16
+        )
         pre_gate = inner_cols(key_part, fast[0])
         pre_up = inner_cols(key_part, fast[1])
         sig_gate = jax.nn.sigmoid(pre_gate)
@@ -336,6 +344,9 @@
         remote(fresh.at[i], fresh.at[i], fresh_send.at[i], fresh_recv.at[i], {"hs": core_peer})
         for i in range(3)
     ]
+    local[7].wait()
+    gate = side[...].astype(jnp.float32)
+    opened[...] = gate * jax.nn.sigmoid(gate)
     hops = list(range(1, layers))
     if hops:
         relay(hops.pop(0))
@@ -347,7 +358,7 @@
         for copy in incoming[:3]:
             copy.wait_recv()
         for j in range(pieces):
-            learn(ctx * tokens + j * piece, j == 0)
+            learn(ctx * tokens + j * piece, rate_ref[:, j * piece : (j + 1) * piece], j == 0)
 
     for j in range(pieces):
         if hops:
@@ -355,9 +366,11 @@
 
         @pl.when(owner)
         def _():
+            if j == 0:
+                incoming[-1].wait_recv()
             incoming[3 + 2 * j].wait_recv()
             incoming[4 + 2 * j].wait_recv()
-            learn(other * tokens + j * piece, False)
+            learn(other * tokens + j * piece, rates[:, j * piece : (j + 1) * piece], False)
 
     for hop in hops:
         relay(hop)
@@ -410,8 +423,7 @@
             copies.append((condition, copy))
 
     pl.when(owner)(cross)
-    for i in (5, 7):
-        local[i].wait()
+    local[5].wait()
     for step in range(layers):
         for other_row in range(2):
             arrived(((depth + step) % layers) * 4 + ((row + other_row) % 2) * 2 + (1 - core))
@@ -447,19 +459,19 @@
 
     size = mixed.shape[2]
     head_count = side.shape[2] // size
-    for seq in range(side.shape[0]):
+    for seq in range(side.shape[1]):
         for head in range(head_count):
             columns = slice(head * size, (head + 1) * size)
             value = mixed[seq * head_count + head].astype(jnp.float32)
             square = jnp.mean(value * value, -1, keepdims=True)
             value = value * lax.rsqrt(square + epsilon) * gain_ref[:, columns]
-            gate = side[seq, :, columns].astype(jnp.float32)
             normed[seq * block_rows : (seq + 1) * block_rows, columns] = (
-                value * (gate * jax.nn.sigmoid(gate))
+                value * opened[:, seq, columns]
             ).astype(jnp.bfloat16)
     result = jnp.dot(normed[...], full[...], preferred_element_type=jnp.float32)
-    for seq in range(side.shape[0]):
-        out_ref[seq] = result[seq * block_rows : (seq + 1) * block_rows].astype(jnp.bfloat16)
+    for seq in range(side.shape[1]):
+        laid[:, seq, :] = result[seq * block_rows : (seq + 1) * block_rows]
+    out_ref[...] = laid[...].astype(jnp.bfloat16)
 
 
 def swapped_body(
@@ -481,31 +493,32 @@
     hidden_size = 2 * fast_gate.shape[1]
     block_rows, seq_count, width = gate_input.shape
     columns = out_weight.shape[1]
-    scaled = (step_rates[0][:, None] * value_rows[0].astype(jnp.float32)).astype(jnp.bfloat16)
-    side = gate_input.transpose(1, 0, 2)
     anywhere = pl.BlockSpec(memory_space=pl.ANY)
     inside = pl.BlockSpec(memory_space=pltpu.VMEM)
     half = jnp.bfloat16
-    result = pl.pallas_call(
+    return pl.pallas_call(
         functools.partial(layer_kernel, layers, pieces),
-        out_shape=jax.ShapeDtypeStruct((seq_count, block_rows, columns), half),
-        in_specs=[anywhere] * 8 + [inside],
+        out_shape=jax.ShapeDtypeStruct((block_rows, seq_count, columns), half),
+        in_specs=[anywhere] * 8 + [inside] * 2,
         out_specs=inside,
         scratch_shapes=[
             pltpu.VMEM((3, hidden_size, size), half),
             pltpu.VMEM((3, hidden_size, size), half),
             pltpu.VMEM((2 * tokens, size), half),
             pltpu.VMEM((2 * tokens, size), half),
+            pltpu.VMEM((1, tokens), jnp.float32),
             pltpu.VMEM((tokens, size), half),
-            pltpu.VMEM((seq_count, block_rows, width), half),
+            pltpu.VMEM((block_rows, seq_count, width), half),
+            pltpu.VMEM((block_rows, seq_count, width), jnp.float32),
             pltpu.VMEM((width, columns), half),
             pltpu.VMEM((3, hidden_size, size), jnp.float32),
             pltpu.VMEM((tokens, size), half),
             pltpu.VMEM((count, block_rows, size), half),
             pltpu.VMEM((seq_count * block_rows, width), half),
+            pltpu.VMEM((block_rows, seq_count, columns), jnp.float32),
             pltpu.SemaphoreType.DMA((8,)),
-            pltpu.SemaphoreType.DMA((4 + 2 * pieces,)),
-            pltpu.SemaphoreType.DMA((4 + 2 * pieces,)),
+            pltpu.SemaphoreType.DMA((5 + 2 * pieces,)),
+            pltpu.SemaphoreType.DMA((5 + 2 * pieces,)),
             pltpu.SemaphoreType.DMA((4 + 6 * (layers - 1) + layers,)),
             pltpu.SemaphoreType.DMA((count,)),
             pltpu.SemaphoreType.DMA((count,)),
@@ -521,14 +534,13 @@
         fast_up,
         fast_down,
         key_rows,
-        scaled,
+        value_rows,
         query_rows,
-        side,
+        gate_input,
         out_weight,
+        step_rates,
         out_gain[None],
     )
-    return result.transpose(1, 0, 2)
-
 
 def solution(mesh):
     def step(*arrays):

time: 53.2 us -> 49.5 us (0.930)
  other arithmetic: 2.04 us -> 0 us
  local copies, waits for them, and re-layouts: 3.62 us -> 1.74 us
    convert_element_type x1 -> x0, other arithmetic: 2.04 us -> none  [swapped_body(): (step_rates[0][:, None] * value_rows[0].astype(jnp.float32)).astype(jnp.b...]
    transpose x1 -> x0, local copies, waits for them, and re-layouts: 1.86 us -> none  [swapped_body(): return result.transpose(1, 0, 2)]
    unnamed x5 -> x1, local copies, waits for them, and re-layouts: 1.77 us -> 1.74 us
where the time goes in v3:
time: 49.5 us; the launch traced here: 48.7 us
  Pallas kernels  47 us (95%)
  local copies, waits for them, and re-layouts  1.74 us (4%)
    pallas_call x1, Pallas kernels, swapped_body(): pl.pallas_call(functools.partial(layer_kernel, layers, pieces), out_shape...  47 us
    unnamed x1, local copies, waits for them, and re-layouts  1.74 us

profile of v3, /device:TPU:13, one launch (start us, length us, event | category | flops | bytes accessed | tf_op | source)
XLA Modules:
  0.0 48.7 jit_solution(11412264238900595824)
XLA Ops:
  0.0 47.0 %shard_map.100 = bf16[32,4,1024]{2,1,0:T(4,128)(2,1)} custom-call(bf16[1,256,512]{2,1,0:T(8,128)(2,1)} %gate_hbm.1, bf16[1,256,512]{2,1,0:T(8,128)(2,1)} %up_hbm.1, bf16[1,256,512]{2,1,0:T(8,128)(2,1)} %down_hbm.1, bf16[1,512,512]{2,1,0:T(8,128)(2,1)} %key_hbm.1, bf16[1,512,512]{2,1,0:T(8,128)(2,1)} %value_hbm.1, bf16[1,512,512]{2,1,0:T(8,128)(2,1)} %query_hbm.1, ...), custom_call_target="tpu_custom_call" | custom-call | tf_op jit(solution)/shard_map/pallas_call | solution.py:499
  47.0 1.7 %copy.12 = bf16[32,4,1024]{2,1,0:T(4,128)(2,1)} copy(bf16[32,4,1024]{2,1,0:T(4,128)(2,1)} %shard_map.100) | data formatting | bytes 524288

commit v4 on v3

--- a/solution.py
+++ b/solution.py
@@ -239,19 +239,26 @@
         remote(source, target(other), ctx_send.at[i], ctx_recv.at[i], {"ctx": other})
         for i, (source, target) in enumerate(swaps)
     ]
-    asked = remote(
-        query_hbm.at[0],
-        queries,
-        ctx_send.at[len(swaps)],
-        ctx_recv.at[len(swaps)],
-        {"ctx": other, "hs": core_peer},
-    )
+    block_rows = tokens // count
+    step_rows = 4 * block_rows
+    asked = []
+    for step in range(layers):
+        span = rows(((depth + step + 1) % layers) * step_rows, step_rows)
+        slot = len(swaps) + step
+        asked.append(
+            remote(
+                query_hbm.at[0, span],
+                queries.at[span],
+                ctx_send.at[slot],
+                ctx_recv.at[slot],
+                {"ctx": other, "hs": core_peer},
+            )
+        )
 
     @pl.when(helper)
     def _():
-        for copy in outgoing[-1:] + outgoing[:-1]:
+        for copy in outgoing[-1:] + outgoing[:-1] + asked:
             copy.start()
-        asked.start()
 
     def full_copy(source, index, slot, device):
         return remote(
@@ -385,15 +392,13 @@
     @pl.when(helper)
     def _():
         cross()
-        asked.wait_recv()
         for copy in handed:
             copy.wait_recv()
 
-    block_rows = tokens // count
-    step_rows = 4 * block_rows
     copies = []
     for step in range(1, layers + 1):
         target = (depth + step) % layers
+        pl.when(helper)(asked[step - 1].wait_recv)
         query_part = queries[rows(target * step_rows, step_rows), :]
         query_gate = inner_cols(query_part, fresh[0])
         query_up = inner_cols(query_part, fresh[1])
@@ -437,10 +442,31 @@
             {"hs": core_peer},
         ).wait_recv()
 
-    for step in range(1, count):
-        head_arrived((me + step) % count)
-    pl.when(helper)(functools.partial(head_arrived, me))
-
+    size = mixed.shape[2]
+    head_count = side.shape[2] // size
+    seqs = side.shape[1]
+    result = None
+    for late in range(2):
+        for half in range(head_count // 2):
+            head = 2 * half + (other if late else ctx)
+            columns = rows(head * size, size)
+            for seq in range(seqs):
+                index = seq * head_count + head
+                guarded(None if late else index != me, functools.partial(head_arrived, index))
+                value = mixed[index].astype(jnp.float32)
+                square = jnp.mean(value * value, -1, keepdims=True)
+                value = value * lax.rsqrt(square + epsilon) * gain_ref[:, columns]
+                normed[seq * block_rows : (seq + 1) * block_rows, columns] = (
+                    value * opened[:, seq, columns]
+                ).astype(jnp.bfloat16)
+            term = jnp.dot(
+                normed[:, columns], full[columns, :], preferred_element_type=jnp.float32
+            )
+            result = term if result is None else result + term
+
+    for seq in range(side.shape[1]):
+        laid[:, seq, :] = result[seq * block_rows : (seq + 1) * block_rows]
+    out_ref[...] = laid[...].astype(jnp.bfloat16)
     for condition, copy in sends + copies:
         guarded(condition, copy.wait_send)
     for _, copy in crossed:
@@ -448,30 +474,13 @@
 
     @pl.when(helper)
     def _():
-        for copy in outgoing:
+        for copy in outgoing + asked:
             copy.wait_send()
-        asked.wait_send()
 
     @pl.when(owner)
     def _():
         for copy in handed:
             copy.wait_send()
-
-    size = mixed.shape[2]
-    head_count = side.shape[2] // size
-    for seq in range(side.shape[1]):
-        for head in range(head_count):
-            columns = slice(head * size, (head + 1) * size)
-            value = mixed[seq * head_count + head].astype(jnp.float32)
-            square = jnp.mean(value * value, -1, keepdims=True)
-            value = value * lax.rsqrt(square + epsilon) * gain_ref[:, columns]
-            normed[seq * block_rows : (seq + 1) * block_rows, columns] = (
-                value * opened[:, seq, columns]
-            ).astype(jnp.bfloat16)
-    result = jnp.dot(normed[...], full[...], preferred_element_type=jnp.float32)
-    for seq in range(side.shape[1]):
-        laid[:, seq, :] = result[seq * block_rows : (seq + 1) * block_rows]
-    out_ref[...] = laid[...].astype(jnp.bfloat16)
 
 
 def swapped_body(
@@ -517,8 +526,8 @@
             pltpu.VMEM((seq_count * block_rows, width), half),
             pltpu.VMEM((block_rows, seq_count, columns), jnp.float32),
             pltpu.SemaphoreType.DMA((8,)),
-            pltpu.SemaphoreType.DMA((5 + 2 * pieces,)),
-            pltpu.SemaphoreType.DMA((5 + 2 * pieces,)),
+            pltpu.SemaphoreType.DMA((4 + 2 * pieces + layers,)),
+            pltpu.SemaphoreType.DMA((4 + 2 * pieces + layers,)),
             pltpu.SemaphoreType.DMA((4 + 6 * (layers - 1) + layers,)),
             pltpu.SemaphoreType.DMA((count,)),
             pltpu.SemaphoreType.DMA((count,)),
@@ -545,6 +554,7 @@
 def solution(mesh):
     def step(*arrays):
         paired = mesh.shape["ctx"] == 2 and mesh.shape["hs"] % 4 == 0
+        paired = paired and arrays[8].shape[2] // arrays[0].shape[2] % 2 == 0
         paired = paired and arrays[0].shape[0] == 1
         return (swapped_body if paired else body)(*arrays)
 

time: 49.5 us -> 50.1 us (1.012); the launches traced: 48.7 us -> 49.9 us
  Pallas kernels: 47 us -> 48.2 us
    pallas_call x1, Pallas kernels: 47 us -> 48.2 us  [swapped_body(): pl.pallas_call(functools.partial(layer_kernel, layers, pieces), out_shape...]
where the time goes in v4:
time: 50.1 us; the launch traced here: 49.9 us
  Pallas kernels  48.2 us (96%)
  local copies, waits for them, and re-layouts  1.74 us (3%)
    pallas_call x1, Pallas kernels, swapped_body(): pl.pallas_call(functools.partial(layer_kernel, layers, pieces), out_shape...  48.2 us
    unnamed x1, local copies, waits for them, and re-layouts  1.74 us

profile of v4, /device:TPU:13, one launch (start us, length us, event | category | flops | bytes accessed | tf_op | source)
XLA Modules:
  0.0 49.9 jit_solution(3486935112334176620)
XLA Ops:
  0.0 48.2 %shard_map.100 = bf16[32,4,1024]{2,1,0:T(4,128)(2,1)} custom-call(bf16[1,256,512]{2,1,0:T(8,128)(2,1)} %gate_hbm.1, bf16[1,256,512]{2,1,0:T(8,128)(2,1)} %up_hbm.1, bf16[1,256,512]{2,1,0:T(8,128)(2,1)} %down_hbm.1, bf16[1,512,512]{2,1,0:T(8,128)(2,1)} %key_hbm.1, bf16[1,512,512]{2,1,0:T(8,128)(2,1)} %value_hbm.1, bf16[1,512,512]{2,1,0:T(8,128)(2,1)} %query_hbm.1, ...), custom_call_target="tpu_custom_call" | custom-call | tf_op jit(solution)/shard_map/pallas_call | solution.py:508
  48.2 1.7 %copy.12 = bf16[32,4,1024]{2,1,0:T(4,128)(2,1)} copy(bf16[32,4,1024]{2,1,0:T(4,128)(2,1)} %shard_map.100) | data formatting | bytes 524288

commit v5 on v3

--- a/solution.py
+++ b/solution.py
@@ -239,19 +239,30 @@
         remote(source, target(other), ctx_send.at[i], ctx_recv.at[i], {"ctx": other})
         for i, (source, target) in enumerate(swaps)
     ]
-    asked = remote(
-        query_hbm.at[0],
-        queries,
-        ctx_send.at[len(swaps)],
-        ctx_recv.at[len(swaps)],
-        {"ctx": other, "hs": core_peer},
-    )
+    block_rows = tokens // count
+    step_rows = 4 * block_rows
+    mid = layers // 2
+    near = (depth // mid) * mid
+    order = [mid - near + (depth + step) % mid for step in range(mid)]
+    order += [near + (depth + step) % mid for step in range(1, mid)] + [depth]
+    asked = []
+    for step in range(layers):
+        span = rows(order[step] * step_rows, step_rows)
+        slot = len(swaps) + step
+        asked.append(
+            remote(
+                query_hbm.at[0, span],
+                queries.at[span],
+                ctx_send.at[slot],
+                ctx_recv.at[slot],
+                {"ctx": other, "hs": core_peer},
+            )
+        )
 
     @pl.when(helper)
     def _():
-        for copy in outgoing[-1:] + outgoing[:-1]:
+        for copy in outgoing[-1:] + outgoing[:-1] + asked:
             copy.start()
-        asked.start()
 
     def full_copy(source, index, slot, device):
         return remote(
@@ -385,15 +396,13 @@
     @pl.when(helper)
     def _():
         cross()
-        asked.wait_recv()
         for copy in handed:
             copy.wait_recv()
 
-    block_rows = tokens // count
-    step_rows = 4 * block_rows
     copies = []
     for step in range(1, layers + 1):
-        target = (depth + step) % layers
+        target = order[step - 1]
+        pl.when(helper)(asked[step - 1].wait_recv)
         query_part = queries[rows(target * step_rows, step_rows), :]
         query_gate = inner_cols(query_part, fresh[0])
         query_up = inner_cols(query_part, fresh[1])
@@ -448,9 +457,8 @@
 
     @pl.when(helper)
     def _():
-        for copy in outgoing:
+        for copy in outgoing + asked:
             copy.wait_send()
-        asked.wait_send()
 
     @pl.when(owner)
     def _():
@@ -517,8 +525,8 @@
             pltpu.VMEM((seq_count * block_rows, width), half),
             pltpu.VMEM((block_rows, seq_count, columns), jnp.float32),
             pltpu.SemaphoreType.DMA((8,)),
-            pltpu.SemaphoreType.DMA((5 + 2 * pieces,)),
-            pltpu.SemaphoreType.DMA((5 + 2 * pieces,)),
+            pltpu.SemaphoreType.DMA((4 + 2 * pieces + layers,)),
+            pltpu.SemaphoreType.DMA((4 + 2 * pieces + layers,)),
             pltpu.SemaphoreType.DMA((4 + 6 * (layers - 1) + layers,)),
             pltpu.SemaphoreType.DMA((count,)),
             pltpu.SemaphoreType.DMA((count,)),
@@ -544,7 +552,7 @@
 
 def solution(mesh):
     def step(*arrays):
-        paired = mesh.shape["ctx"] == 2 and mesh.shape["hs"] % 4 == 0
+        paired = mesh.shape["ctx"] == 2 and mesh.shape["hs"] % 8 == 0
         paired = paired and arrays[0].shape[0] == 1
         return (swapped_body if paired else body)(*arrays)
 

time: 49.5 us -> 48.7 us (0.984)
  Pallas kernels: 47 us -> 46.4 us
    pallas_call x1, Pallas kernels: 47 us -> 46.4 us  [swapped_body(): pl.pallas_call(functools.partial(layer_kernel, layers, pieces), out_shape...]
where the time goes in v5:
time: 48.7 us; the launch traced here: 48.1 us
  Pallas kernels  46.4 us (95%)
  local copies, waits for them, and re-layouts  1.74 us (4%)
    pallas_call x1, Pallas kernels, swapped_body(): pl.pallas_call(functools.partial(layer_kernel, layers, pieces), out_shape...  46.4 us
    unnamed x1, local copies, waits for them, and re-layouts  1.74 us

profile of v5, /device:TPU:13, one launch (start us, length us, event | category | flops | bytes accessed | tf_op | source)
XLA Modules:
  0.0 48.1 jit_solution(1029923405943678039)
XLA Ops:
  0.0 46.4 %shard_map.100 = bf16[32,4,1024]{2,1,0:T(4,128)(2,1)} custom-call(bf16[1,256,512]{2,1,0:T(8,128)(2,1)} %gate_hbm.1, bf16[1,256,512]{2,1,0:T(8,128)(2,1)} %up_hbm.1, bf16[1,256,512]{2,1,0:T(8,128)(2,1)} %down_hbm.1, bf16[1,512,512]{2,1,0:T(8,128)(2,1)} %key_hbm.1, bf16[1,512,512]{2,1,0:T(8,128)(2,1)} %value_hbm.1, bf16[1,512,512]{2,1,0:T(8,128)(2,1)} %query_hbm.1, ...), custom_call_target="tpu_custom_call" | custom-call | tf_op jit(solution)/shard_map/pallas_call | solution.py:507
  46.4 1.7 %copy.12 = bf16[32,4,1024]{2,1,0:T(4,128)(2,1)} copy(bf16[32,4,1024]{2,1,0:T(4,128)(2,1)} %shard_map.100) | data formatting | bytes 524288

commit v6 on v5

--- a/solution.py
+++ b/solution.py
@@ -395,7 +395,6 @@
 
     @pl.when(helper)
     def _():
-        cross()
         for copy in handed:
             copy.wait_recv()
 
@@ -431,7 +430,7 @@
             guarded(condition, copy.start)
             copies.append((condition, copy))
 
-    pl.when(owner)(cross)
+    cross()
     local[5].wait()
     for step in range(layers):
         for other_row in range(2):

time: 48.7 us -> 48.8 us (level)
  no operation moved by 1% of the time
where the time goes in v6:
time: 48.8 us; the launch traced here: 48 us
  Pallas kernels  46.3 us (95%)
  local copies, waits for them, and re-layouts  1.74 us (4%)
    pallas_call x1, Pallas kernels, swapped_body(): pl.pallas_call(functools.partial(layer_kernel, layers, pieces), out_shape...  46.3 us
    unnamed x1, local copies, waits for them, and re-layouts  1.74 us

profile of v6, /device:TPU:13, one launch (start us, length us, event | category | flops | bytes accessed | tf_op | source)
XLA Modules:
  0.0 48.0 jit_solution(16331759647884893064)
XLA Ops:
  0.0 46.3 %shard_map.100 = bf16[32,4,1024]{2,1,0:T(4,128)(2,1)} custom-call(bf16[1,256,512]{2,1,0:T(8,128)(2,1)} %gate_hbm.1, bf16[1,256,512]{2,1,0:T(8,128)(2,1)} %up_hbm.1, bf16[1,256,512]{2,1,0:T(8,128)(2,1)} %down_hbm.1, bf16[1,512,512]{2,1,0:T(8,128)(2,1)} %key_hbm.1, bf16[1,512,512]{2,1,0:T(8,128)(2,1)} %value_hbm.1, bf16[1,512,512]{2,1,0:T(8,128)(2,1)} %query_hbm.1, ...), custom_call_target="tpu_custom_call" | custom-call | tf_op jit(solution)/shard_map/pallas_call | solution.py:506
  46.3 1.7 %copy.12 = bf16[32,4,1024]{2,1,0:T(4,128)(2,1)} copy(bf16[32,4,1024]{2,1,0:T(4,128)(2,1)} %shard_map.100) | data formatting | bytes 524288
